TPU v7x, 32 devices: a whole 2x2x4 slice. The times are simulated.
32 devices in a mesh: groups: 2 (over y), dp: 4 (over z), mp: 2 (over x), layer: 2 (over core).
Axes of the slice: x: 2, y: 2, z: 4, core: 2. Of those that a mesh axis runs over, the one named last changes fastest.
Arguments:
- acts: bfloat16 [2, 4096, 8192], P('layer', ('groups', 'dp'), 'mp'), parts along dimension 1, may hold values from -6 to 6
- grads: bfloat16 [2, 4096, 28672], P('layer', ('groups', 'dp'), 'mp'), parts along dimension 1, may hold values from -6 to 6
- query_left: bfloat16 [2, 8192, 512], P('layer', ('mp', 'dp'), 'groups'), parts along dimension 2, may hold values from -0.0625 to 0.0625
- query_right: bfloat16 [2, 28672, 512], P('layer', ('mp', 'dp'), 'groups'), parts along dimension 2, may hold values from -0.03125 to 0.03125
- seq_len: int32 [16], P(('groups', 'dp')), parts along dimension 0, may hold values from 1 to 256, 1024 in all
Outputs:
- scores: float32 [2, 16, 32], P('layer', ('groups', 'dp')), parts along dimension 1
There are 2 independent parts, one for each index of `groups`. A program takes and returns all parts, laid end to end along the dimension named above; each array names one. Nothing has to cross between parts.
Inputs may be any that keep to these rules, and one draw needn't show every extreme that they name: `seq_len`: every sequence has at least one live token and some sequence has exactly 256.
All inputs are finite; a program needn't handle non-finite values. No bound on the sum of `seq_len` on one device may be relied on, other than what follows from the above.
Results may differ from a plain program's by a relative error of at most 0.0003.
Values may be sent and summed in bfloat16 or wider, within the bound.
A program may use at most 64 MiB of HBM per device.

v0:
```python
import functools
import math

import jax
import jax.numpy as jnp
from jax import lax
from jax.experimental import pallas as pl
from jax.experimental.pallas import tpu as pltpu
from jax.sharding import PartitionSpec as P

RANK = 8
LEN = 256
T = 256
LATE = 1
OFF = 11
MESH = pl.DeviceIdType.MESH


def seq_scores(proj_acts, proj_grads, live_mask):
    seq_count, seq_span = live_mask.shape
    product = (proj_acts * proj_grads).reshape(seq_count, seq_span, proj_acts.shape[1])
    summed = jnp.sum(product * live_mask[:, :, None], axis=1)
    return jnp.sum(summed.reshape(seq_count, -1, RANK), axis=2) / math.sqrt(RANK * LEN)


def on_device(acts, grads, query_left, query_right, seq_len):
    row_count = acts.shape[1]
    seq_count = seq_len.shape[0]
    seq_span = row_count // seq_count
    positions = lax.broadcasted_iota(jnp.int32, (seq_count, seq_span), 1)
    live_mask = (positions < seq_len[:, None]).astype(jnp.float32)
    proj_acts = jnp.dot(
        acts[0],
        lax.all_gather(query_left[0], "dp", axis=0, tiled=True),
        preferred_element_type=jnp.float32,
    )
    proj_grads = jnp.dot(
        grads[0],
        lax.all_gather(query_right[0], "dp", axis=0, tiled=True),
        preferred_element_type=jnp.float32,
    )
    share_acts = lax.psum_scatter(proj_acts, "mp", scatter_dimension=1, tiled=True)
    share_grads = lax.psum_scatter(proj_grads, "mp", scatter_dimension=1, tiled=True)
    share_scores = seq_scores(share_acts, share_grads, live_mask)
    return lax.all_gather(share_scores, "mp", axis=1, tiled=True)[None]


def line_kernel(
    left_rows, right_rows, acts, grads, ql, qr, seq_len, out,
    xa, wg, xb, acc, xacc, ra, live_a, got_a, psum, ret, sums, rsums, cp,
    s_in, s_out, s_fwd_a, s_fwd_b, s_fwd_c, s_x, r_w, r_x, s_r, r_r,
):
    z = lax.axis_index("dp")
    m = lax.axis_index("mp")
    end = (z == 0) | (z == 3)
    inner = (z == 1) | (z == 2)
    step = jnp.where(z < 2, 1, -1)
    ahead = jnp.clip(z + step, 0, 3)
    behind = jnp.clip(z - step, 0, 3)
    far = jnp.clip(z + 2 * step, 0, 3)
    last = jnp.clip(z + 3 * step, 0, 3)
    peer = 1 - m

    a_cols = 4 * left_rows
    rows = left_rows + right_rows
    a_pieces, pieces = left_rows // T, rows // T
    keep = pieces - OFF
    half = acc.shape[1] // 2

    locals_ = [
        pltpu.make_async_copy(acts.at[0], xa.at[:, pl.ds(0, a_cols)], cp.at[0]),
        pltpu.make_async_copy(grads.at[0], xa.at[:, pl.ds(a_cols, 4 * right_rows)], cp.at[1]),
        pltpu.make_async_copy(ql.at[0], wg.at[pl.ds(pl.multiple_of(z * rows, T), left_rows)], cp.at[2]),
        pltpu.make_async_copy(
            qr.at[0], wg.at[pl.ds(pl.multiple_of(z * rows + left_rows, T), right_rows)], cp.at[3]
        ),
    ]

    barrier = pltpu.get_barrier_semaphore()
    pl.semaphore_signal(barrier, inc=1, device_id={"mp": peer}, device_id_type=MESH)
    pl.semaphore_signal(barrier, inc=1, device_id={"dp": ahead}, device_id_type=MESH)

    @pl.when(inner)
    def _():
        pl.semaphore_signal(barrier, inc=1, device_id={"dp": behind}, device_id_type=MESH)
        pl.semaphore_wait(barrier, 3)

    @pl.when(end)
    def _():
        pl.semaphore_wait(barrier, 2)

    def slot(owner, k):
        return wg.at[pl.ds(pl.multiple_of((owner * pieces + k) * T, T), T)]

    def piece_source(k):
        if k < a_pieces:
            return ql.at[0, pl.ds(k * T, T)]
        return qr.at[0, pl.ds((k - a_pieces) * T, T)]

    def send_own(k, to, sem):
        return pltpu.make_async_remote_copy(
            src_ref=piece_source(k), dst_ref=slot(z, k), send_sem=sem.at[k],
            recv_sem=r_w.at[z * pieces + k], device_id={"dp": to}, device_id_type=MESH,
        )

    def pass_on(owner, k, to, sem):
        return pltpu.make_async_remote_copy(
            src_ref=slot(owner, k), dst_ref=slot(owner, k), send_sem=sem.at[k],
            recv_sem=r_w.at[owner * pieces + k], device_id={"dp": to}, device_id_type=MESH,
        )

    def arrived(owner, k):
        pass_on(owner, k, ahead, s_fwd_a).wait_recv()

    def send_x(i):
        first = a_cols * 0 + ahead * right_rows + (keep - a_pieces + i) * T
        return pltpu.make_async_remote_copy(
            src_ref=grads.at[0, :, pl.ds(pl.multiple_of(first, T), T)], dst_ref=xb.at[i],
            send_sem=s_x.at[i], recv_sem=r_x.at[i], device_id={"dp": ahead}, device_id_type=MESH,
        )

    def multiply(owner, k):
        is_a = k < a_pieces
        col = jnp.where(
            is_a, owner * left_rows + k * T, a_cols + owner * right_rows + (k - a_pieces) * T
        )
        which = jnp.where(is_a, 0, 1)
        acc[which] += jnp.dot(
            xa[:, pl.ds(pl.multiple_of(col, T), T)], slot(owner, k)[...],
            preferred_element_type=jnp.float32,
        )

    def to_peer(src, dst, i):
        return pltpu.make_async_remote_copy(
            src_ref=src, dst_ref=dst, send_sem=s_r.at[i], recv_sem=r_r.at[i],
            device_id={"mp": peer}, device_id_type=MESH,
        )

    mine = pl.ds(pl.multiple_of(m * half, half), half)
    share_a = to_peer(acc.at[0], ra, 0)
    share_x = to_peer(got_a.at[mine], got_a.at[mine], 1)
    share_s = to_peer(sums, rsums, 2)

    def lend_a():
        return pltpu.make_async_remote_copy(
            src_ref=live_a.at[mine], dst_ref=got_a.at[mine], send_sem=s_r.at[3], recv_sem=r_r.at[3],
            device_id={"dp": ahead}, device_id_type=MESH,
        )

    def give_back():
        return pltpu.make_async_remote_copy(
            src_ref=psum, dst_ref=ret, send_sem=s_r.at[4], recv_sem=r_r.at[4],
            device_id={"dp": behind}, device_id_type=MESH,
        )

    def finish_a():
        share_a.wait_recv()
        row = lax.broadcasted_iota(jnp.int32, ra.shape, 0)
        stop = jnp.where(row < half, seq_len[0], half + seq_len[1])
        live_a[...] = jnp.where(row < stop, acc[0] + ra[...], 0.0)

    def row_sum(x):
        return jnp.broadcast_to(jnp.sum(x, axis=0, keepdims=True), sums.shape)

    def seq_sums(a_ref, g_ref):
        at = lax.broadcasted_iota(jnp.int32, sums.shape, 0)
        return jnp.where(
            at == 0,
            row_sum(a_ref[:half] * g_ref[:half]),
            row_sum(a_ref[half:] * g_ref[half:]),
        )

    @pl.when(end)
    def _():
        for k in range(pieces):
            send_own(k, ahead, s_in).start()
        for i in range(OFF - LATE):
            send_x(i).start()

    @pl.when(inner)
    def _():
        for k in range(pieces):
            send_own(k, ahead, s_in).start()
            if k < keep:
                send_own(k, behind, s_out).start()

    for c in locals_:
        c.start()
    acc[...] = jnp.zeros_like(acc)
    for c in locals_:
        c.wait()

    @pl.when(end)
    def _():
        @pl.loop(0, pieces)
        def _(k):
            multiply(z, k)

        @pl.loop(0, keep)
        def _(k):
            arrived(ahead, k)
            multiply(ahead, k)

        @pl.loop(0, pieces)
        def _(k):
            arrived(far, k)
            multiply(far, k)

        @pl.loop(0, pieces)
        def _(k):
            arrived(last, k)
            multiply(last, k)

            @pl.when(k == a_pieces - 1)
            def _():
                share_a.start()

            @pl.when(k == a_pieces + 4)
            def _():
                finish_a()

            @pl.when(k == a_pieces + 5)
            def _():
                lend_a().start()
                for i in range(OFF - LATE, OFF):
                    send_x(i).start()

    @pl.when(inner)
    def _():
        xacc[...] = jnp.zeros_like(xacc)

        def take_x(i):
            pltpu.make_async_remote_copy(
                src_ref=xb.at[i], dst_ref=xb.at[i], send_sem=s_x.at[i], recv_sem=r_x.at[i],
                device_id={"dp": behind}, device_id_type=MESH,
            ).wait_recv()
            xacc[...] += jnp.dot(
                xb[i], slot(z, keep + i)[...], preferred_element_type=jnp.float32
            )

        @pl.loop(0, pieces)
        def _(k):
            arrived(ahead, k)
            pass_on(ahead, k, behind, s_fwd_a).start()
            arrived(behind, k)
            pass_on(behind, k, ahead, s_fwd_b).start()
            multiply(ahead, k)
            multiply(behind, k)
            multiply(z, k)

        @pl.loop(0, pieces)
        def _(k):
            arrived(far, k)
            pass_on(far, k, behind, s_fwd_c).start()
            multiply(far, k)

            @pl.when(k == a_pieces - 1)
            def _():
                share_a.start()

        finish_a()

        @pl.loop(0, OFF - LATE)
        def _(i):
            take_x(i)

        lend_a().wait_recv()
        share_x.start()
        share_x.wait_recv()

        @pl.loop(OFF - LATE, OFF)
        def _(i):
            take_x(i)

        psum[...] = seq_sums(got_a, xacc)
        give_back().start()

    sums[...] = seq_sums(live_a, acc.at[1])

    @pl.when(end)
    def _():
        give_back().wait_recv()
        sums[...] += ret[...]

    share_s.start()
    share_s.wait_recv()
    both = sums[...] + rsums[...]
    n_q = out.shape[2]
    qi = lax.broadcasted_iota(jnp.int32, (both.shape[1], n_q), 0)
    qj = lax.broadcasted_iota(jnp.int32, (both.shape[1], n_q), 1)
    pick = ((qi >= qj * RANK) & (qi < (qj + 1) * RANK)).astype(jnp.float32)
    scores = jnp.dot(
        both, pick, preferred_element_type=jnp.float32, precision=lax.Precision.HIGHEST
    )
    out[0] = scores[: out.shape[1]]

    share_a.wait_send()
    share_s.wait_send()

    @pl.when(end)
    def _():
        for i in range(OFF):
            send_x(i).wait_send()
        lend_a().wait_send()
        for k in range(pieces):
            send_own(k, ahead, s_in).wait_send()

    @pl.when(inner)
    def _():
        for k in range(pieces):
            send_own(k, ahead, s_in).wait_send()
            if k < keep:
                send_own(k, behind, s_out).wait_send()
            pass_on(ahead, k, behind, s_fwd_a).wait_send()
            pass_on(behind, k, ahead, s_fwd_b).wait_send()
            pass_on(far, k, behind, s_fwd_c).wait_send()
        share_x.wait_send()
        give_back().wait_send()


def on_line(acts, grads, query_left, query_right, seq_len):
    rows, cols = acts.shape[1], query_left.shape[2]
    left_rows, right_rows = query_left.shape[1], query_right.shape[1]
    pieces = (left_rows + right_rows) // T
    dma, f32, bf16 = pltpu.SemaphoreType.DMA, jnp.float32, jnp.bfloat16
    anywhere = pl.BlockSpec(memory_space=pl.ANY)
    return pl.pallas_call(
        functools.partial(line_kernel, left_rows, right_rows),
        out_shape=jax.ShapeDtypeStruct((1, seq_len.shape[0], cols // RANK), f32),
        in_specs=[anywhere] * 4 + [pl.BlockSpec(memory_space=pltpu.SMEM)],
        out_specs=pl.BlockSpec(memory_space=pltpu.VMEM),
        scratch_shapes=[
            pltpu.VMEM((rows, acts.shape[2] + grads.shape[2]), bf16),
            pltpu.VMEM((4 * (left_rows + right_rows), cols), bf16),
            pltpu.VMEM((OFF, rows, T), bf16),
            pltpu.VMEM((2, rows, cols), f32),
            pltpu.VMEM((rows, cols), f32),
            pltpu.VMEM((rows, cols), f32),
            pltpu.VMEM((rows, cols), f32),
            pltpu.VMEM((rows, cols), f32),
            pltpu.VMEM((8, cols), f32),
            pltpu.VMEM((8, cols), f32),
            pltpu.VMEM((8, cols), f32),
            pltpu.VMEM((8, cols), f32),
            dma((4,)),
            dma((pieces,)),
            dma((pieces,)),
            dma((pieces,)),
            dma((pieces,)),
            dma((pieces,)),
            dma((OFF,)),
            dma((4 * pieces,)),
            dma((OFF,)),
            dma((5,)),
            dma((5,)),
        ],
        compiler_params=pltpu.CompilerParams(
            collective_id=0, has_side_effects=True, vmem_limit_bytes=60 * 1024 * 1024
        ),
    )(acts, grads, query_left, query_right, seq_len)


def fits_line(mesh, acts, query_left, query_right, seq_len):
    rows = acts.shape[1]
    pieces_g = query_right.shape[1] // T
    return (
        mesh.shape["dp"] == 4
        and mesh.shape["mp"] == 2
        and seq_len.shape[0] == 2
        and rows % 32 == 0
        and query_left.shape[1] % T == 0
        and query_right.shape[1] % T == 0
        and query_left.shape[1] >= T
        and pieces_g >= OFF
    )


def solution(mesh):
    def body(acts, grads, query_left, query_right, seq_len):
        if fits_line(mesh, acts, query_left, query_right, seq_len):
            summed = on_line(acts, grads, query_left, query_right, seq_len)
            return summed / math.sqrt(RANK * LEN)
        return on_device(acts, grads, query_left, query_right, seq_len)

    return jax.shard_map(
        body,
        mesh=mesh,
        in_specs=(
            P("layer", ("groups", "dp"), "mp"),
            P("layer", ("groups", "dp"), "mp"),
            P("layer", ("mp", "dp"), "groups"),
            P("layer", ("mp", "dp"), "groups"),
            P(("groups", "dp")),
        ),
        out_specs=P("layer", ("groups", "dp"), None),
        check_vma=False,
    )
```

profile of v0, /device:TPU:0, one launch (start us, length us, event | category | flops | bytes accessed | tf_op | source)
XLA Modules:
  0.0 134.2 jit_solution(12333495074312101419)
XLA Ops:
  0.0 133.0 %shard_map.55 = f32[1,2,32]{2,1,0:T(2,128)} custom-call(bf16[1,512,4096]{2,1,0:T(8,128)(2,1)} %acts.1, bf16[1,512,14336]{2,1,0:T(8,128)(2,1)} %grads.1, bf16[1,1024,256]{2,1,0:T(8,128)(2,1)} %ql.1, bf16[1,3584,256]{2,1,0:T(8,128)(2,1)} %qr.1, s32[2]{0:T(128)} %seq_len.1), custom_call_target="tpu_custom_call" | custom-call | tf_op jit(solution)/shard_map/pallas_call | solution.py:327
  133.0 1.2 broadcast_multiply_fusion
where the time goes:
time: 134 us
  Pallas kernels  133 us (99%)
    pallas_call x1, Pallas kernels, on_line(): pl.pallas_call(functools.partial(line_kernel, left_rows, right_rows), out...  133 us

commit v1 on v0

--- a/solution.py
+++ b/solution.py
@@ -46,8 +46,8 @@
 
 
 def line_kernel(
-    left_rows, right_rows, acts, grads, ql, qr, seq_len, out,
-    xa, wg, xb, acc, xacc, ra, live_a, got_a, psum, ret, sums, rsums, cp,
+    left_rows, right_rows, acts, grads, ql, qr, seq_hbm, out,
+    xa, wg, xb, acc, xacc, ra, live_a, got_a, psum, ret, sums, rsums, seq_len, cp,
     s_in, s_out, s_fwd_a, s_fwd_b, s_fwd_c, s_x, r_w, r_x, s_r, r_r,
 ):
     z = lax.axis_index("dp")
@@ -76,6 +76,8 @@
         ),
     ]
 
+    lens = pltpu.make_async_copy(seq_hbm, seq_len, cp.at[4])
+
     barrier = pltpu.get_barrier_semaphore()
     pl.semaphore_signal(barrier, inc=1, device_id={"mp": peer}, device_id_type=MESH)
     pl.semaphore_signal(barrier, inc=1, device_id={"dp": ahead}, device_id_type=MESH)
@@ -83,6 +85,13 @@
     @pl.when(inner)
     def _():
         pl.semaphore_signal(barrier, inc=1, device_id={"dp": behind}, device_id_type=MESH)
+
+    lens.start()
+    for c in locals_:
+        c.start()
+
+    @pl.when(inner)
+    def _():
         pl.semaphore_wait(barrier, 3)
 
     @pl.when(end)
@@ -184,9 +193,8 @@
             if k < keep:
                 send_own(k, behind, s_out).start()
 
-    for c in locals_:
-        c.start()
     acc[...] = jnp.zeros_like(acc)
+    lens.wait()
     for c in locals_:
         c.wait()
 
@@ -323,11 +331,11 @@
     left_rows, right_rows = query_left.shape[1], query_right.shape[1]
     pieces = (left_rows + right_rows) // T
     dma, f32, bf16 = pltpu.SemaphoreType.DMA, jnp.float32, jnp.bfloat16
-    anywhere = pl.BlockSpec(memory_space=pl.ANY)
+    anywhere = pl.BlockSpec(memory_space=pltpu.HBM)
     return pl.pallas_call(
         functools.partial(line_kernel, left_rows, right_rows),
-        out_shape=jax.ShapeDtypeStruct((1, seq_len.shape[0], cols // RANK), f32),
-        in_specs=[anywhere] * 4 + [pl.BlockSpec(memory_space=pltpu.SMEM)],
+        out_shape=pltpu.VMEM((1, seq_len.shape[0], cols // RANK), f32),
+        in_specs=[anywhere] * 5,
         out_specs=pl.BlockSpec(memory_space=pltpu.VMEM),
         scratch_shapes=[
             pltpu.VMEM((rows, acts.shape[2] + grads.shape[2]), bf16),
@@ -342,7 +350,8 @@
             pltpu.VMEM((8, cols), f32),
             pltpu.VMEM((8, cols), f32),
             pltpu.VMEM((8, cols), f32),
-            dma((4,)),
+            pltpu.SMEM((seq_len.shape[0],), jnp.int32),
+            dma((5,)),
             dma((pieces,)),
             dma((pieces,)),
             dma((pieces,)),

time: 134 us -> 132 us (0.985)
  no operation moved by 1% of the time
where the time goes in v1:
time: 132 us
  Pallas kernels  132 us (100%)
    pallas_call x1, Pallas kernels, on_line(): pl.pallas_call(functools.partial(line_kernel, left_rows, right_rows), out...  132 us

profile of v1, /device:TPU:0, one launch (start us, length us, event | category | flops | bytes accessed | tf_op | source)
XLA Modules:
  0.0 132.3 jit_solution(57146800105074672)
XLA Ops:
  0.0 131.7 %shard_map.55 = f32[1,2,32]{2,1,0:T(2,128)S(1)} custom-call(bf16[1,512,4096]{2,1,0:T(8,128)(2,1)} %acts.1, bf16[1,512,14336]{2,1,0:T(8,128)(2,1)} %grads.1, bf16[1,1024,256]{2,1,0:T(8,128)(2,1)} %ql.1, bf16[1,3584,256]{2,1,0:T(8,128)(2,1)} %qr.1, s32[2]{0:T(128)} %seq_hbm.1), custom_call_target="tpu_custom_call" | custom-call | tf_op jit(solution)/shard_map/pallas_call | solution.py:335
  131.7 0.6 broadcast_multiply_fusion

commit v2 on v1

--- a/solution.py
+++ b/solution.py
@@ -11,7 +11,7 @@
 RANK = 8
 LEN = 256
 T = 256
-LATE = 1
+LATE = 2
 OFF = 11
 MESH = pl.DeviceIdType.MESH
 
@@ -48,7 +48,7 @@
 def line_kernel(
     left_rows, right_rows, acts, grads, ql, qr, seq_hbm, out,
     xa, wg, xb, acc, xacc, ra, live_a, got_a, psum, ret, sums, rsums, seq_len, cp,
-    s_in, s_out, s_fwd_a, s_fwd_b, s_fwd_c, s_x, r_w, r_x, s_r, r_r,
+    s_w, s_x, r_w, r_x, s_r, r_r,
 ):
     z = lax.axis_index("dp")
     m = lax.axis_index("mp")
@@ -64,7 +64,7 @@
     a_cols = 4 * left_rows
     rows = left_rows + right_rows
     a_pieces, pieces = left_rows // T, rows // T
-    keep = pieces - OFF
+    keep, early = pieces - OFF, OFF - LATE
     half = acc.shape[1] // 2
 
     locals_ = [
@@ -101,6 +101,9 @@
     def slot(owner, k):
         return wg.at[pl.ds(pl.multiple_of((owner * pieces + k) * T, T), T)]
 
+    def landing(owner, k, at):
+        return r_w.at[((owner - at + 3) % 4) * pieces + k]
+
     def piece_source(k):
         if k < a_pieces:
             return ql.at[0, pl.ds(k * T, T)]
@@ -108,24 +111,36 @@
 
     def send_own(k, to, sem):
         return pltpu.make_async_remote_copy(
-            src_ref=piece_source(k), dst_ref=slot(z, k), send_sem=sem.at[k],
-            recv_sem=r_w.at[z * pieces + k], device_id={"dp": to}, device_id_type=MESH,
+            src_ref=piece_source(k), dst_ref=slot(z, k), send_sem=s_w.at[sem],
+            recv_sem=landing(z, k, to), device_id={"dp": to}, device_id_type=MESH,
         )
 
     def pass_on(owner, k, to, sem):
         return pltpu.make_async_remote_copy(
-            src_ref=slot(owner, k), dst_ref=slot(owner, k), send_sem=sem.at[k],
-            recv_sem=r_w.at[owner * pieces + k], device_id={"dp": to}, device_id_type=MESH,
+            src_ref=slot(owner, k), dst_ref=slot(owner, k), send_sem=s_w.at[sem],
+            recv_sem=landing(owner, k, to), device_id={"dp": to}, device_id_type=MESH,
         )
 
     def arrived(owner, k):
-        pass_on(owner, k, ahead, s_fwd_a).wait_recv()
+        pltpu.make_async_remote_copy(
+            src_ref=slot(owner, k), dst_ref=slot(owner, k), send_sem=s_w.at[0],
+            recv_sem=landing(owner, k, z), device_id={"dp": ahead}, device_id_type=MESH,
+        ).wait_recv()
+
+    def all_sent(sem, count, to):
+        whole = wg.at[pl.ds(0, count * T)]
+        pltpu.make_async_remote_copy(
+            src_ref=whole, dst_ref=whole, send_sem=s_w.at[sem], recv_sem=r_w.at[0],
+            device_id={"dp": to}, device_id_type=MESH,
+        ).wait_send()
 
     def send_x(i):
-        first = a_cols * 0 + ahead * right_rows + (keep - a_pieces + i) * T
-        return pltpu.make_async_remote_copy(
-            src_ref=grads.at[0, :, pl.ds(pl.multiple_of(first, T), T)], dst_ref=xb.at[i],
-            send_sem=s_x.at[i], recv_sem=r_x.at[i], device_id={"dp": ahead}, device_id_type=MESH,
+        skip, count = (0, early) if i == 0 else (early + i - 1, 1)
+        first = ahead * right_rows + (keep - a_pieces + skip) * T
+        return pltpu.make_async_remote_copy(
+            src_ref=grads.at[0, :, pl.ds(pl.multiple_of(first, T), count * T)],
+            dst_ref=xb.at[:, pl.ds(skip * T, count * T)], send_sem=s_x.at[i], recv_sem=r_x.at[i],
+            device_id={"dp": ahead}, device_id_type=MESH,
         )
 
     def multiply(owner, k):
@@ -182,16 +197,15 @@
     @pl.when(end)
     def _():
         for k in range(pieces):
-            send_own(k, ahead, s_in).start()
-        for i in range(OFF - LATE):
-            send_x(i).start()
+            send_own(k, ahead, 0).start()
+        send_x(0).start()
 
     @pl.when(inner)
     def _():
         for k in range(pieces):
-            send_own(k, ahead, s_in).start()
+            send_own(k, ahead, 0).start()
             if k < keep:
-                send_own(k, behind, s_out).start()
+                send_own(k, behind, 1).start()
 
     acc[...] = jnp.zeros_like(acc)
     lens.wait()
@@ -230,28 +244,33 @@
             @pl.when(k == a_pieces + 5)
             def _():
                 lend_a().start()
-                for i in range(OFF - LATE, OFF):
+                for i in range(1, LATE + 1):
                     send_x(i).start()
 
     @pl.when(inner)
     def _():
         xacc[...] = jnp.zeros_like(xacc)
 
-        def take_x(i):
+        def x_here(i):
+            skip, count = (0, early) if i == 0 else (early + i - 1, 1)
+            part = xb.at[:, pl.ds(skip * T, count * T)]
             pltpu.make_async_remote_copy(
-                src_ref=xb.at[i], dst_ref=xb.at[i], send_sem=s_x.at[i], recv_sem=r_x.at[i],
+                src_ref=part, dst_ref=part, send_sem=s_x.at[i], recv_sem=r_x.at[i],
                 device_id={"dp": behind}, device_id_type=MESH,
             ).wait_recv()
+
+        def take_x(i):
             xacc[...] += jnp.dot(
-                xb[i], slot(z, keep + i)[...], preferred_element_type=jnp.float32
+                xb[:, pl.ds(pl.multiple_of(i * T, T), T)], slot(z, keep + i)[...],
+                preferred_element_type=jnp.float32,
             )
 
         @pl.loop(0, pieces)
         def _(k):
             arrived(ahead, k)
-            pass_on(ahead, k, behind, s_fwd_a).start()
+            pass_on(ahead, k, behind, 2).start()
             arrived(behind, k)
-            pass_on(behind, k, ahead, s_fwd_b).start()
+            pass_on(behind, k, ahead, 3).start()
             multiply(ahead, k)
             multiply(behind, k)
             multiply(z, k)
@@ -259,7 +278,7 @@
         @pl.loop(0, pieces)
         def _(k):
             arrived(far, k)
-            pass_on(far, k, behind, s_fwd_c).start()
+            pass_on(far, k, behind, 4).start()
             multiply(far, k)
 
             @pl.when(k == a_pieces - 1)
@@ -268,7 +287,9 @@
 
         finish_a()
 
-        @pl.loop(0, OFF - LATE)
+        x_here(0)
+
+        @pl.loop(0, early)
         def _(i):
             take_x(i)
 
@@ -276,9 +297,9 @@
         share_x.start()
         share_x.wait_recv()
 
-        @pl.loop(OFF - LATE, OFF)
-        def _(i):
-            take_x(i)
+        for i in range(1, LATE + 1):
+            x_here(i)
+            take_x(early + i - 1)
 
         psum[...] = seq_sums(got_a, xacc)
         give_back().start()
@@ -307,21 +328,18 @@
 
     @pl.when(end)
     def _():
-        for i in range(OFF):
+        for i in range(LATE + 1):
             send_x(i).wait_send()
         lend_a().wait_send()
-        for k in range(pieces):
-            send_own(k, ahead, s_in).wait_send()
+        all_sent(0, pieces, ahead)
 
     @pl.when(inner)
     def _():
-        for k in range(pieces):
-            send_own(k, ahead, s_in).wait_send()
-            if k < keep:
-                send_own(k, behind, s_out).wait_send()
-            pass_on(ahead, k, behind, s_fwd_a).wait_send()
-            pass_on(behind, k, ahead, s_fwd_b).wait_send()
-            pass_on(far, k, behind, s_fwd_c).wait_send()
+        all_sent(0, pieces, ahead)
+        all_sent(1, keep, behind)
+        all_sent(2, pieces, behind)
+        all_sent(3, pieces, ahead)
+        all_sent(4, pieces, behind)
         share_x.wait_send()
         give_back().wait_send()
 
@@ -340,7 +358,7 @@
         scratch_shapes=[
             pltpu.VMEM((rows, acts.shape[2] + grads.shape[2]), bf16),
             pltpu.VMEM((4 * (left_rows + right_rows), cols), bf16),
-            pltpu.VMEM((OFF, rows, T), bf16),
+            pltpu.VMEM((rows, OFF * T), bf16),
             pltpu.VMEM((2, rows, cols), f32),
             pltpu.VMEM((rows, cols), f32),
             pltpu.VMEM((rows, cols), f32),
@@ -352,14 +370,10 @@
             pltpu.VMEM((8, cols), f32),
             pltpu.SMEM((seq_len.shape[0],), jnp.int32),
             dma((5,)),
-            dma((pieces,)),
-            dma((pieces,)),
-            dma((pieces,)),
-            dma((pieces,)),
-            dma((pieces,)),
-            dma((OFF,)),
-            dma((4 * pieces,)),
-            dma((OFF,)),
+            dma((5,)),
+            dma((LATE + 1,)),
+            dma((3 * pieces,)),
+            dma((LATE + 1,)),
             dma((5,)),
             dma((5,)),
         ],

time: 132 us -> 131 us (level)
  no operation moved by 1% of the time
where the time goes in v2:
time: 131 us
  Pallas kernels  131 us (100%)
    pallas_call x1, Pallas kernels, on_line(): pl.pallas_call(functools.partial(line_kernel, left_rows, right_rows), out...  131 us

profile of v2, /device:TPU:0, one launch (start us, length us, event | category | flops | bytes accessed | tf_op | source)
XLA Modules:
  0.0 131.1 jit_solution(3304263928501764094)
XLA Ops:
  0.0 130.5 %shard_map.55 = f32[1,2,32]{2,1,0:T(2,128)S(1)} custom-call(bf16[1,512,4096]{2,1,0:T(8,128)(2,1)} %acts.1, bf16[1,512,14336]{2,1,0:T(8,128)(2,1)} %grads.1, bf16[1,1024,256]{2,1,0:T(8,128)(2,1)} %ql.1, bf16[1,3584,256]{2,1,0:T(8,128)(2,1)} %qr.1, s32[2]{0:T(128)} %seq_hbm.1), custom_call_target="tpu_custom_call" | custom-call | tf_op jit(solution)/shard_map/pallas_call | solution.py:353
  130.5 0.6 broadcast_multiply_fusion

commit v3 on v2

--- a/solution.py
+++ b/solution.py
@@ -51,6 +51,7 @@
     s_w, s_x, r_w, r_x, s_r, r_r,
 ):
     z = lax.axis_index("dp")
+    yields = lax.axis_index("layer") == 1
     m = lax.axis_index("mp")
     end = (z == 0) | (z == 3)
     inner = (z == 1) | (z == 2)
@@ -67,15 +68,14 @@
     keep, early = pieces - OFF, OFF - LATE
     half = acc.shape[1] // 2
 
-    locals_ = [
-        pltpu.make_async_copy(acts.at[0], xa.at[:, pl.ds(0, a_cols)], cp.at[0]),
+    acts_in = pltpu.make_async_copy(acts.at[0], xa.at[:, pl.ds(0, a_cols)], cp.at[0])
+    others_in = [
         pltpu.make_async_copy(grads.at[0], xa.at[:, pl.ds(a_cols, 4 * right_rows)], cp.at[1]),
         pltpu.make_async_copy(ql.at[0], wg.at[pl.ds(pl.multiple_of(z * rows, T), left_rows)], cp.at[2]),
         pltpu.make_async_copy(
             qr.at[0], wg.at[pl.ds(pl.multiple_of(z * rows + left_rows, T), right_rows)], cp.at[3]
         ),
     ]
-
     lens = pltpu.make_async_copy(seq_hbm, seq_len, cp.at[4])
 
     barrier = pltpu.get_barrier_semaphore()
@@ -87,7 +87,8 @@
         pl.semaphore_signal(barrier, inc=1, device_id={"dp": behind}, device_id_type=MESH)
 
     lens.start()
-    for c in locals_:
+    acts_in.start()
+    for c in others_in:
         c.start()
 
     @pl.when(inner)
@@ -194,6 +195,10 @@
             row_sum(a_ref[half:] * g_ref[half:]),
         )
 
+    @pl.when(yields)
+    def _():
+        acts_in.wait()
+
     @pl.when(end)
     def _():
         for k in range(pieces):
@@ -209,8 +214,12 @@
 
     acc[...] = jnp.zeros_like(acc)
     lens.wait()
-    for c in locals_:
+    for c in others_in:
         c.wait()
+
+    @pl.when(jnp.logical_not(yields))
+    def _():
+        acts_in.wait()
 
     @pl.when(end)
     def _():

time: 131 us -> 132 us (level)
  no operation moved by 1% of the time
where the time goes in v3:
time: 132 us
  Pallas kernels  131 us (99%)
    pallas_call x1, Pallas kernels, on_line(): pl.pallas_call(functools.partial(line_kernel, left_rows, right_rows), out...  131 us

profile of v3, /device:TPU:0, one launch (start us, length us, event | category | flops | bytes accessed | tf_op | source)
XLA Modules:
  0.0 132.0 jit_solution(16114729638936767774)
XLA Ops:
  0.0 131.4 %shard_map.55 = f32[1,2,32]{2,1,0:T(2,128)S(1)} custom-call(bf16[1,512,4096]{2,1,0:T(8,128)(2,1)} %acts.1, bf16[1,512,14336]{2,1,0:T(8,128)(2,1)} %grads.1, bf16[1,1024,256]{2,1,0:T(8,128)(2,1)} %ql.1, bf16[1,3584,256]{2,1,0:T(8,128)(2,1)} %qr.1, s32[2]{0:T(128)} %seq_hbm.1), custom_call_target="tpu_custom_call" | custom-call | tf_op jit(solution)/shard_map/pallas_call | solution.py:362
  131.4 0.6 broadcast_multiply_fusion

commit v4 on v2

--- a/solution.py
+++ b/solution.py
@@ -67,15 +67,16 @@
     keep, early = pieces - OFF, OFF - LATE
     half = acc.shape[1] // 2
 
-    locals_ = [
+    rows_in = [
         pltpu.make_async_copy(acts.at[0], xa.at[:, pl.ds(0, a_cols)], cp.at[0]),
         pltpu.make_async_copy(grads.at[0], xa.at[:, pl.ds(a_cols, 4 * right_rows)], cp.at[1]),
+    ]
+    own_in = [
         pltpu.make_async_copy(ql.at[0], wg.at[pl.ds(pl.multiple_of(z * rows, T), left_rows)], cp.at[2]),
         pltpu.make_async_copy(
             qr.at[0], wg.at[pl.ds(pl.multiple_of(z * rows + left_rows, T), right_rows)], cp.at[3]
         ),
     ]
-
     lens = pltpu.make_async_copy(seq_hbm, seq_len, cp.at[4])
 
     barrier = pltpu.get_barrier_semaphore()
@@ -87,7 +88,7 @@
         pl.semaphore_signal(barrier, inc=1, device_id={"dp": behind}, device_id_type=MESH)
 
     lens.start()
-    for c in locals_:
+    for c in own_in:
         c.start()
 
     @pl.when(inner)
@@ -104,14 +105,9 @@
     def landing(owner, k, at):
         return r_w.at[((owner - at + 3) % 4) * pieces + k]
 
-    def piece_source(k):
-        if k < a_pieces:
-            return ql.at[0, pl.ds(k * T, T)]
-        return qr.at[0, pl.ds((k - a_pieces) * T, T)]
-
     def send_own(k, to, sem):
         return pltpu.make_async_remote_copy(
-            src_ref=piece_source(k), dst_ref=slot(z, k), send_sem=s_w.at[sem],
+            src_ref=slot(z, k), dst_ref=slot(z, k), send_sem=s_w.at[sem],
             recv_sem=landing(z, k, to), device_id={"dp": to}, device_id_type=MESH,
         )
 
@@ -194,6 +190,9 @@
             row_sum(a_ref[half:] * g_ref[half:]),
         )
 
+    for c in own_in:
+        c.wait()
+
     @pl.when(end)
     def _():
         for k in range(pieces):
@@ -207,9 +206,11 @@
             if k < keep:
                 send_own(k, behind, 1).start()
 
+    for c in rows_in:
+        c.start()
     acc[...] = jnp.zeros_like(acc)
     lens.wait()
-    for c in locals_:
+    for c in rows_in:
         c.wait()
 
     @pl.when(end)

time: 131 us -> 131 us (level)
  no operation moved by 1% of the time
where the time goes in v4:
time: 131 us
  Pallas kernels  131 us (100%)
    pallas_call x1, Pallas kernels, on_line(): pl.pallas_call(functools.partial(line_kernel, left_rows, right_rows), out...  131 us

profile of v4, /device:TPU:0, one launch (start us, length us, event | category | flops | bytes accessed | tf_op | source)
XLA Modules:
  0.0 131.2 jit_solution(3494906506941179603)
XLA Ops:
  0.0 130.7 %shard_map.55 = f32[1,2,32]{2,1,0:T(2,128)S(1)} custom-call(bf16[1,512,4096]{2,1,0:T(8,128)(2,1)} %acts.1, bf16[1,512,14336]{2,1,0:T(8,128)(2,1)} %grads.1, bf16[1,1024,256]{2,1,0:T(8,128)(2,1)} %ql.1, bf16[1,3584,256]{2,1,0:T(8,128)(2,1)} %qr.1, s32[2]{0:T(128)} %seq_hbm.1), custom_call_target="tpu_custom_call" | custom-call | tf_op jit(solution)/shard_map/pallas_call | solution.py:354
  130.7 0.6 broadcast_multiply_fusion

commit v5 on v2

--- a/solution.py
+++ b/solution.py
@@ -312,6 +312,14 @@
         sums[...] += ret[...]
 
     share_s.start()
+
+    @pl.when(end)
+    def _():
+        for i in range(LATE + 1):
+            send_x(i).wait_send()
+        lend_a().wait_send()
+        all_sent(0, pieces, ahead)
+
     share_s.wait_recv()
     both = sums[...] + rsums[...]
     n_q = out.shape[2]
@@ -321,17 +329,10 @@
     scores = jnp.dot(
         both, pick, preferred_element_type=jnp.float32, precision=lax.Precision.HIGHEST
     )
-    out[0] = scores[: out.shape[1]]
+    out[0] = scores[: out.shape[1]] / math.sqrt(RANK * LEN)
 
     share_a.wait_send()
     share_s.wait_send()
-
-    @pl.when(end)
-    def _():
-        for i in range(LATE + 1):
-            send_x(i).wait_send()
-        lend_a().wait_send()
-        all_sent(0, pieces, ahead)
 
     @pl.when(inner)
     def _():
@@ -401,8 +402,7 @@
 def solution(mesh):
     def body(acts, grads, query_left, query_right, seq_len):
         if fits_line(mesh, acts, query_left, query_right, seq_len):
-            summed = on_line(acts, grads, query_left, query_right, seq_len)
-            return summed / math.sqrt(RANK * LEN)
+            return on_line(acts, grads, query_left, query_right, seq_len)
         return on_device(acts, grads, query_left, query_right, seq_len)
 
     return jax.shard_map(

time: 131 us -> 131 us (level)
  no operation moved by 1% of the time
where the time goes in v5:
time: 131 us
  Pallas kernels  131 us (100%)
    pallas_call x1, Pallas kernels, on_line(): pl.pallas_call(functools.partial(line_kernel, left_rows, right_rows), out...  131 us

profile of v5, /device:TPU:0, one launch (start us, length us, event | category | flops | bytes accessed | tf_op | source)
XLA Modules:
  0.0 131.1 jit_solution(4505892805195991010)
XLA Ops:
  0.0 130.5 %shard_map.55 = f32[1,2,32]{2,1,0:T(2,128)S(1)} custom-call(bf16[1,512,4096]{2,1,0:T(8,128)(2,1)} %acts.1, bf16[1,512,14336]{2,1,0:T(8,128)(2,1)} %grads.1, bf16[1,1024,256]{2,1,0:T(8,128)(2,1)} %ql.1, bf16[1,3584,256]{2,1,0:T(8,128)(2,1)} %qr.1, s32[2]{0:T(128)} %seq_hbm.1), custom_call_target="tpu_custom_call" | custom-call | tf_op jit(solution)/shard_map/pallas_call | solution.py:354
  130.5 0.6 copy.7

commit v6 on v5

--- a/solution.py
+++ b/solution.py
@@ -329,7 +329,7 @@
     scores = jnp.dot(
         both, pick, preferred_element_type=jnp.float32, precision=lax.Precision.HIGHEST
     )
-    out[0] = scores[: out.shape[1]] / math.sqrt(RANK * LEN)
+    out[0] = scores[: out.shape[1]]
 
     share_a.wait_send()
     share_s.wait_send()
@@ -402,7 +402,8 @@
 def solution(mesh):
     def body(acts, grads, query_left, query_right, seq_len):
         if fits_line(mesh, acts, query_left, query_right, seq_len):
-            return on_line(acts, grads, query_left, query_right, seq_len)
+            summed = on_line(acts, grads, query_left, query_right, seq_len)
+            return summed / math.sqrt(RANK * LEN)
         return on_device(acts, grads, query_left, query_right, seq_len)
 
     return jax.shard_map(

time: 131 us -> 131 us (level)
  no operation moved by 1% of the time
where the time goes in v6:
time: 131 us
  Pallas kernels  131 us (100%)
    pallas_call x1, Pallas kernels, on_line(): pl.pallas_call(functools.partial(line_kernel, left_rows, right_rows), out...  131 us

profile of v6, /device:TPU:0, one launch (start us, length us, event | category | flops | bytes accessed | tf_op | source)
XLA Modules:
  0.0 131.1 jit_solution(15957291300669497474)
XLA Ops:
  0.0 130.5 %shard_map.55 = f32[1,2,32]{2,1,0:T(2,128)S(1)} custom-call(bf16[1,512,4096]{2,1,0:T(8,128)(2,1)} %acts.1, bf16[1,512,14336]{2,1,0:T(8,128)(2,1)} %grads.1, bf16[1,1024,256]{2,1,0:T(8,128)(2,1)} %ql.1, bf16[1,3584,256]{2,1,0:T(8,128)(2,1)} %qr.1, s32[2]{0:T(128)} %seq_hbm.1), custom_call_target="tpu_custom_call" | custom-call | tf_op jit(solution)/shard_map/pallas_call | solution.py:354
  130.5 0.6 broadcast_multiply_fusion
